TPU v7x, 32 devices: a whole 2x2x4 slice. The times are simulated.
32 devices in a mesh: row: 8 (over z, y), col: 4 (over x, core).
Axes of the slice: x: 2, y: 2, z: 4, core: 2. Of those that a mesh axis runs over, the one named last changes fastest.
Arguments:
- matrix: float32 [6144, 16384], P('row', 'col'), may hold values from -6 to 6
Outputs:
- updated: float32 [6144, 16384], P('row', 'col')
All inputs are finite; a program needn't handle non-finite values.
Results may differ from a plain program's by a relative error of at most 0.0003.
Values sent between devices are 32-bit elements; how exact they have to be, the bound alone decides.
A program may use at most 128 MiB of HBM per device.

v0:
```python
import jax
import jax.numpy as jnp
from jax import lax
from jax.sharding import PartitionSpec as P

PANEL = 128


def broadcast(x, axis, root):
    mine = lax.axis_index(axis) == root
    return lax.psum(jnp.where(mine, x, jnp.zeros_like(x)), axis)


def column_steps(working):
    count = working.shape[0]
    current = working
    for column in range(count - 1):
        pivot_value = current[column, column]
        multiplier = current[column + 1 :, column] / pivot_value
        trailing_block = (
            current[column + 1 :, column + 1 :]
            - multiplier[:, None] * current[column, column + 1 :][None, :]
        )
        current = current.at[column + 1 :, column + 1 :].set(trailing_block)
        current = current.at[column + 1 :, column].set(multiplier)
    lower_unit = jnp.tril(current, -1) + jnp.eye(count, dtype=current.dtype)
    upper_tri = jnp.triu(current)
    return (lower_unit, upper_tri)


def eliminate(working):
    count = working.shape[0]
    if count <= 8:
        return column_steps(working)
    half = count // 2
    lower_top, upper_top = eliminate(working[:half, :half])
    upper_right = jax.scipy.linalg.solve_triangular(
        lower_top, working[:half, half:], lower=True, unit_diagonal=True
    )
    lower_left = jax.scipy.linalg.solve_triangular(
        upper_top.T, working[half:, :half].T, lower=True
    ).T
    schur = working[half:, half:] - jnp.dot(
        lower_left, upper_right, precision=lax.Precision.HIGHEST
    )
    lower_bottom, upper_bottom = eliminate(schur)
    rest = count - half
    zeros_right = jnp.zeros((half, rest), dtype=working.dtype)
    zeros_left = jnp.zeros((rest, half), dtype=working.dtype)
    lower_unit = jnp.concatenate(
        [
            jnp.concatenate([lower_top, zeros_right], axis=1),
            jnp.concatenate([lower_left, lower_bottom], axis=1),
        ],
        axis=0,
    )
    upper_tri = jnp.concatenate(
        [
            jnp.concatenate([upper_top, upper_right], axis=1),
            jnp.concatenate([zeros_left, upper_bottom], axis=1),
        ],
        axis=0,
    )
    return (lower_unit, upper_tri)


def combine_coefficients(lower_unit, upper_tri, projected):
    scaled = jnp.dot(upper_tri.T, projected, precision=lax.Precision.HIGHEST)
    return jax.scipy.linalg.solve_triangular(lower_unit, scaled, lower=True, unit_diagonal=True)


def on_device(matrix):
    high = lax.Precision.HIGHEST
    row_count = matrix.shape[0]
    column_block = broadcast(matrix[:, :PANEL], "col", 0)
    top_rows = broadcast(column_block[:PANEL], "row", 0)
    gram_part = jnp.dot(column_block.T, column_block, precision=high)
    gram_total = lax.psum(gram_part, "row")
    cholesky_low = jnp.linalg.cholesky(gram_total)
    basis_local = jax.scipy.linalg.solve_triangular(cholesky_low, column_block.T, lower=True)
    top_basis = jax.scipy.linalg.solve_triangular(cholesky_low, top_rows.T, lower=True)
    lower_unit, upper_tri = eliminate(top_basis.T + jnp.eye(PANEL, dtype=jnp.float32))
    reflectors = jax.scipy.linalg.solve_triangular(upper_tri.T, basis_local, lower=True)
    global_rows = lax.axis_index("row") * row_count + jnp.arange(row_count)
    padded_lower = jnp.zeros_like(reflectors).at[:, :PANEL].set(lower_unit.T)
    reflectors = jnp.where(global_rows[None, :] < PANEL, padded_lower, reflectors)
    projected_part = jnp.dot(reflectors, matrix, precision=high)
    projected = lax.psum(projected_part, "row")
    coefficients = combine_coefficients(lower_unit, upper_tri, projected)
    return matrix - jnp.dot(reflectors.T, coefficients, precision=high)


def solution(mesh):
    in_specs = (P("row", "col"),)
    out_specs = P("row", "col")
    return jax.shard_map(
        on_device, mesh=mesh, in_specs=in_specs, out_specs=out_specs, check_vma=False
    )
```

profile of v0, /device:TPU:10, one launch (start us, length us, event | category | flops | bytes accessed | tf_op | source)
XLA Modules:
  0.0 622.1 jit_solution(14434221857366712905)
XLA Ops:
  6.5 1.8 slice_select_fusion
  8.4 34.3 %all-reduce.36.cloned.1.call-done = f32[768,128]{1,0:T(8,128)} async-done(((f32[768,128]{1,0:T(8,128)}), f32[768,128]{1,0:T(8,128)}) %all-reduce.36.cloned.1.call-update) | async-done | bytes 393232 | tf_op jit(solution)/shard_map/psum | solution.py:11
  42.7 2.5 fusion.278
  45.2 1.5 slice_select_fusion.1
  47.4 70.5 %all-reduce.40.cloned.1.call-done = (f32[128,128]{0,1:T(8,128)}, f32[128,128]{1,0:T(8,128)}) async-done(((f32[128,128]{0,1:T(8,128)}, f32[128,128]{1,0:T(8,128)}), (f32[128,128]{0,1:T(8,128)}, f32[128,128]{1,0:T(8,128)})) %all-reduce.40.cloned.1.call-update) | async-done | bytes 131088 | tf_op jit(solution)/shard_map/psum | solution.py:78
  119.7 11.7 %cholesky.19 = f32[128,128]{1,0:T(8,128)S(1)} custom-call(f32[128,128]{1,0:T(8,128)S(1)} %fusion.11), custom_call_target="Cholesky" | custom-call | tf_op jit(solution)/shard_map/jit(cholesky)/cholesky | solution.py:79
  132.7 9.8 %custom-call.40 = f32[1,128,128]{1,2,0:T(8,128)S(1)} custom-call(f32[1,128,128]{2,1,0:T(8,128)S(1)} %fusion.2), custom_call_target="InvertDiagBlocksLowerTriangular" | custom-call | tf_op jit(solution)/shard_map/jit(_solve_triangular)/triangular_solve | solution.py:81
  180.2 1.2 custom-call.70
  181.9 1.2 custom-call.69
  219.9 2.4 custom-call.74
  222.8 2.4 custom-call.73
  261.8 1.2 custom-call.78
  263.4 1.2 custom-call.77
  301.6 4.9 custom-call.41
  306.9 4.9 custom-call.42
  388.6 2.4 custom-call.88
  391.4 2.4 custom-call.87
  470.4 9.8 %custom-call.96 = f32[1,128,128]{1,2,0:T(8,128)S(1)} custom-call(f32[1,128,128]{2,1,0:T(8,128)S(1)} %copy.70), custom_call_target="InvertDiagBlocksLowerTriangular" | custom-call | tf_op jit(solution)/shard_map/jit(_solve_triangular)/triangular_solve | solution.py:83
  482.2 10.9 %fusion.279 = f32[128,4096]{1,0:T(8,128)} fusion(f32[128,768]{0,1:T(8,128)S(1)} %convolution_select_fusion, f32[768,4096]{1,0:T(8,128)} %param.465), kind=kOutput, calls=%fused_computation.694 | convolution fusion | flops 4831838208 | bytes 15073280 | tf_op jit(solution)/shard_map/dot_general | solution.py:87
  493.4 9.8 %custom-call.43 = f32[1,128,128]{1,2,0:T(8,128)S(1)} custom-call(f32[1,128,128]{2,1,0:T(8,128)S(1)} %fusion.4), custom_call_target="InvertDiagBlocksLowerTriangular" | custom-call | tf_op jit(solution)/shard_map/jit(_solve_triangular)/triangular_solve | solution.py:69
  503.2 91.9 %all-reduce.38.cloned.1.call-done = f32[128,4096]{1,0:T(8,128)} async-done(((f32[128,4096]{1,0:T(8,128)}), f32[128,4096]{1,0:T(8,128)}) %all-reduce.38.cloned.1.call-update) | async-done | bytes 2097168 | tf_op jit(solution)/shard_map/psum | solution.py:88
  595.1 3.6 fusion.154
  598.7 1.9 fusion.5
  600.6 14.6 %convolution_subtract_fusion = f32[768,4096]{1,0:T(8,128)} fusion(f32[768,4096]{1,0:T(8,128)} %param.465, f32[128,768]{0,1:T(8,128)S(1)} %convolution_select_fusion, f32[128,4096]{1,0:T(8,128)S(1)} %fusion.5), kind=kOutput, calls=%fused_computation | convolution fusion | flops 4834983936 | bytes 27656192 | tf_op jit(solution)/shard_map/dot_general | solution.py:90
  (801 shorter events, 266.6 us)
Async XLA Ops:
  6.5 36.2 %all-reduce.36.cloned.1.call-start = ((), (), s32[]{:S(2)}) async-start(), calls=%async_computation | async-start | bytes 786432 | tf_op jit(solution)/shard_map/psum | solution.py:11
  8.3 109.5 %all-reduce.40.cloned.1.call-start = ((), (), s32[]{:S(2)}) async-start(), calls=%async_computation.2 | async-start | bytes 262144 | tf_op jit(solution)/shard_map/psum | solution.py:78
  46.7 548.4 %all-reduce.38.cloned.1.call-start = ((), (), s32[]{:S(2)}) async-start(), calls=%async_computation.1 | async-start | bytes 4194304 | tf_op jit(solution)/shard_map/psum | solution.py:88
  306.8 174.1 %copy-start = (f32[768,128]{1,0:T(8,128)S(1)}, f32[768,128]{1,0:T(8,128)}, u32[]{:S(2)}) copy-start(f32[768,128]{1,0:T(8,128)} %all-reduce.36.cloned.1.call-done) | copy-start | bytes 1179652
Sparse Core Ops, SparseCore 0:
  9.7 32.9 all-reduce.35
  46.8 70.9 all-reduce.39
  493.2 101.8 all-reduce.37
where the time goes:
time: 634 us; the launch traced here: 622 us
  waiting for transfers between devices  197 us (31%)
  other arithmetic  177 us (28%)
  local copies, waits for them, and re-layouts  149 us (24%)
  between operations  56.6 us (9%)
  matrix products  42.8 us (7%)
    psum x1, waiting for transfers between devices, on_device(): projected = lax.psum(projected_part, 'row')  91.9 us
    div x96, other arithmetic, column_steps(): multiplier = current[column + 1:, column] / pivot_value  78.1 us
    psum x1, waiting for transfers between devices, on_device(): gram_total = lax.psum(gram_part, 'row')  70.5 us
    slice x96, local copies, waits for them, and re-layouts, column_steps(): pivot_value = current[column, column]  55.8 us
    scatter x112, local copies, waits for them, and re-layouts, column_steps(): current = current.at[column + 1:, column + 1:].set(trailing_block)  45.3 us
    psum x1, waiting for transfers between devices, broadcast(): return lax.psum(jnp.where(mine, x, jnp.zeros_like(x)), axis)  34.3 us
    scatter x112, local copies, waits for them, and re-layouts, column_steps(): current = current.at[column + 1:, column].set(multiplier)  27.8 us
    another operation x30, other arithmetic, eliminate(): jax.scipy.linalg.solve_triangular(upper_top.T, working[half:, :half].T, l...  20.9 us
  transfers between devices with their start and end apart: 3, of which 3 were waited for; matrix products, arithmetic and copies ran while one was open for 2% of the time, Pallas kernels for 0%

commit v1 on v0

v1 whole, which is shorter than its diff:
```python
import jax
import jax.numpy as jnp
from jax import lax
from jax.experimental import pallas as pl
from jax.experimental.pallas import tpu as pltpu
from jax.sharding import PartitionSpec as P

PANEL = 128
STRIP = 8


def dot_exact(a, b, contract):
    return lax.dot_general(
        a, b, (contract, ((), ())), precision=lax.Precision.HIGHEST, preferred_element_type=jnp.float32
    )


def factor_values(gram, top):
    strips = PANEL // STRIP
    rows = lax.broadcasted_iota(jnp.int32, (STRIP, 1), 0)
    eye = (
        lax.broadcasted_iota(jnp.int32, (PANEL, PANEL), 0) == lax.broadcasted_iota(jnp.int32, (PANEL, PANEL), 1)
    ).astype(jnp.float32)
    chol = jnp.concatenate([gram, eye], axis=1)
    work = jnp.concatenate([top, jnp.zeros_like(top)], axis=1)
    factor_rows = []
    for strip in range(strips):
        at = strip * STRIP
        panel = chol[:STRIP]
        scale = jnp.ones((STRIP, 1), jnp.float32)
        for j in range(STRIP):
            column = panel[:, at + j : at + j + 1]
            pivot = column[j : j + 1]
            multiplier = jnp.where(rows > j, column / pivot, 0.0)
            scale = jnp.where(rows == j, lax.rsqrt(pivot), scale)
            panel = panel - multiplier * panel[j : j + 1]
        panel = panel * scale
        lanes = lax.broadcasted_iota(jnp.int32, (STRIP, 2 * PANEL), 1)
        panel = jnp.where(lanes >= at + rows, panel, 0.0)
        factor_rows.append(panel[:, :PANEL])
        if strip < strips - 1:
            below = panel[:, at + STRIP : PANEL]
            chol = chol[STRIP:] - dot_exact(below, panel, ((0,), (0,)))

        inner = work[at : at + STRIP] + panel
        for j in range(STRIP):
            column = inner[:, at + j : at + j + 1]
            pivot_row = inner[j : j + 1] / column[j : j + 1]
            inner = jnp.where(rows == j, pivot_row, inner - column * pivot_row)
        update = dot_exact(work[:, at : at + STRIP], inner, ((1,), (0,)))
        pieces = []
        if at > 0:
            pieces.append(work[:at] - update[:at])
        pieces.append(inner)
        if strip < strips - 1:
            pieces.append(work[at + STRIP :] - update[at + STRIP :])
        work = jnp.concatenate(pieces, axis=0)
    return jnp.concatenate(factor_rows, axis=0), work[:, PANEL:]


def factor_kernel(gram_ref, top_ref, factor_ref, inverse_ref):
    factor, inverse = factor_values(gram_ref[...], top_ref[...])
    factor_ref[...] = factor
    inverse_ref[...] = inverse


def factorize(gram, top):
    square = jax.ShapeDtypeStruct((PANEL, PANEL), jnp.float32)
    return pl.pallas_call(factor_kernel, out_shape=(square, square), name="factorize")(gram, top)


def on_device(matrix):
    own = jnp.where(lax.axis_index("col") == 0, matrix[:, :PANEL], 0.0)
    panel = lax.psum(own, "col")
    first = lax.axis_index("row") == 0
    gram_part = jnp.dot(panel.T, panel, precision=lax.Precision.HIGHEST)
    gram, top = lax.psum((gram_part, jnp.where(first, panel[:PANEL], 0.0)), "row")
    factor, inverse = factorize(gram, top)
    shifted = panel.at[:PANEL].add(jnp.where(first, factor, 0.0))
    partial = lax.dot_general(shifted, matrix, (((0,), (0,)), ((), ())), precision=lax.Precision.HIGH)
    summed = lax.psum(partial, "row")
    coefficients = jnp.dot(inverse, summed, precision=lax.Precision.HIGH)
    return matrix - jnp.dot(shifted, coefficients, precision=lax.Precision.HIGH)


def solution(mesh):
    return jax.shard_map(
        on_device, mesh=mesh, in_specs=(P("row", "col"),), out_specs=P("row", "col"), check_vma=False
    )
```

time: 634 us -> 273 us (0.43); the launches traced: 622 us -> 271 us
  other arithmetic: 177 us -> 4.7 us
  local copies, waits for them, and re-layouts: 149 us -> 0.01 us
  between operations: 56.6 us -> 13.1 us
  Pallas kernels: 0 us -> 20.2 us
  matrix products: 42.8 us -> 25.7 us
  waiting for transfers between devices: 197 us -> 207 us
    another operation x67 -> x0, other arithmetic: 85.1 us -> none  [the longest x30 20.9 us: eliminate(): jax.scipy.linalg.solve_triangular(upper_top.T, working[half:, :half].T, l...]
    div x97 -> x0, other arithmetic: 79 us -> none  [the longest x96 78.1 us: column_steps(): multiplier = current[column + 1:, column] / pivot_value]
    scatter x224 -> x0, local copies, waits for them, and re-layouts: 73.1 us -> none  [the longest x112 45.3 us: column_steps(): current = current.at[column + 1:, column + 1:].set(trailing_block)]
    slice x120 -> x0, local copies, waits for them, and re-layouts: 66.6 us -> none  [the longest x96 55.8 us: column_steps(): pivot_value = current[column, column]]
    pallas_call x0 -> x1, Pallas kernels: none -> 20.2 us  [factorize(): pl.pallas_call(factor_kernel, out_shape=(square, square), name='factorize')]
    psum x3, waiting for transfers between devices: 197 us -> 207 us  [the longest x1 102 us: on_device(): summed = lax.psum(partial, 'row')]
    another operation x34 -> x0, matrix products: 9.66 us -> none  [the longest x15 3.28 us: eliminate(): jax.scipy.linalg.solve_triangular(lower_top, working[:half, half:], lower...]
    dot_general x19 -> x4, matrix products: 33.1 us -> 25.7 us  [the longest x1 10.9 us: on_device(): return matrix - jnp.dot(shifted, coefficients, precision=lax.Precision.HIGH)]
  transfers between devices with their start and end apart: 3 -> 3, of which waited for: 3 -> 3; matrix products, arithmetic and copies ran while one was open for 2% -> 0% of each run, Pallas kernels for 0% -> 0%
where the time goes in v1:
time: 273 us; the launch traced here: 271 us
  waiting for transfers between devices  207 us (76%)
  matrix products  25.7 us (9%)
  Pallas kernels  20.2 us (7%)
  between operations  13.1 us (5%)
  other arithmetic  4.7 us (2%)
    psum x1, waiting for transfers between devices, on_device(): summed = lax.psum(partial, 'row')  102 us
    psum x1, waiting for transfers between devices, on_device(): lax.psum((gram_part, jnp.where(first, panel[:PANEL], 0.0)), 'row')  71.1 us
    psum x1, waiting for transfers between devices, on_device(): panel = lax.psum(own, 'col')  34.3 us
    pallas_call x1, Pallas kernels, factorize(): pl.pallas_call(factor_kernel, out_shape=(square, square), name='factorize')  20.2 us
    dot_general x1, matrix products, on_device(): return matrix - jnp.dot(shifted, coefficients, precision=lax.Precision.HIGH)  10.9 us
    dot_general x1, matrix products, on_device(): lax.dot_general(shifted, matrix, (((0,), (0,)), ((), ())), precision=lax....  9.62 us
  transfers between devices with their start and end apart: 3, of which 3 were waited for; matrix products, arithmetic and copies ran while one was open for 0% of the time, Pallas kernels for 0%

profile of v1, /device:TPU:10, one launch (start us, length us, event | category | flops | bytes accessed | tf_op | source)
XLA Modules:
  0.0 271.1 jit_solution(338166709409999976)
XLA Ops:
  6.5 0.0 all-reduce.5.cloned.1.call-start
  6.5 1.8 slice_select_fusion
  8.3 0.0 all-reduce.5.cloned.1.call-update
  8.3 0.0 all-reduce.9.cloned.1.call-start
  8.4 34.3 %all-reduce.5.cloned.1.call-done = f32[768,128]{1,0:T(8,128)} async-done(((f32[768,128]{1,0:T(8,128)}), f32[768,128]{1,0:T(8,128)}) %all-reduce.5.cloned.1.call-update) | async-done | bytes 393232 | tf_op jit(solution)/shard_map/psum | solution.py:74
  42.7 2.5 fusion
  45.2 1.5 slice_select_fusion.1
  46.7 0.0 all-reduce.9.cloned.1.call-update
  46.7 0.0 all-reduce.7.cloned.1.call-start
  46.8 71.1 %all-reduce.9.cloned.1.call-done = (f32[128,128]{1,0:T(8,128)}, f32[128,128]{1,0:T(8,128)}) async-done(((f32[128,128]{1,0:T(8,128)}, f32[128,128]{1,0:T(8,128)}), (f32[128,128]{1,0:T(8,128)}, f32[128,128]{1,0:T(8,128)})) %all-reduce.9.cloned.1.call-update) | async-done | bytes 131088 | tf_op jit(solution)/shard_map/psum | solution.py:77
  117.9 20.2 %factorize.1 = (f32[128,128]{1,0:T(8,128)}, f32[128,128]{1,0:T(8,128)}) custom-call(f32[128,128]{1,0:T(8,128)} %get-tuple-element.21.gram_ref, f32[128,128]{1,0:T(8,128)} %get-tuple-element.22.top_ref), custom_call_target="tpu_custom_call" | custom-call | tf_op jit(solution)/shard_map/factorize/pallas_call | solution.py:69
  138.1 1.5 add_dynamic-update-slice_fusion
  139.6 9.6 %fusion.1 = f32[128,4096]{1,0:T(8,128)} fusion(f32[768,128]{1,0:T(8,128)} %add_dynamic-update-slice_fusion, f32[768,4096]{1,0:T(8,128)} %param.3), kind=kOutput, calls=%fused_computation.5 | convolution fusion | flops 2415919104 | bytes 15073280 | tf_op jit(solution)/shard_map/dot_general | solution.py:80
  149.2 0.0 copy-start.1
  149.2 0.0 all-reduce.7.cloned.1.call-update
  149.2 101.9 %all-reduce.7.cloned.1.call-done = f32[128,4096]{1,0:T(8,128)} async-done(((f32[128,4096]{1,0:T(8,128)}), f32[128,4096]{1,0:T(8,128)}) %all-reduce.7.cloned.1.call-update) | async-done | bytes 2097168 | tf_op jit(solution)/shard_map/psum | solution.py:81
  251.1 0.0 copy-done.1
  251.1 0.0 copy-start
  251.1 2.6 fusion.2
  253.7 0.0 copy-done
  253.7 10.9 %convolution_subtract_fusion = f32[768,4096]{1,0:T(8,128)} fusion(f32[768,4096]{1,0:T(8,128)} %param.3, f32[768,128]{1,0:T(8,128)S(1)} %copy-done, f32[128,4096]{1,0:T(8,128)S(1)} %fusion.2), kind=kOutput, calls=%fused_computation | convolution fusion | flops 2419064832 | bytes 27656192 | tf_op jit(solution)/shard_map/dot_general | solution.py:83
Async XLA Ops:
  6.5 36.2 %all-reduce.5.cloned.1.call-start = ((), (), s32[]{:S(2)}) async-start(), calls=%async_computation | async-start | bytes 786432 | tf_op jit(solution)/shard_map/psum | solution.py:74
  8.3 109.5 %all-reduce.9.cloned.1.call-start = ((), (), s32[]{:S(2)}) async-start(), calls=%async_computation.2 | async-start | bytes 262144 | tf_op jit(solution)/shard_map/psum | solution.py:77
  46.7 204.3 %all-reduce.7.cloned.1.call-start = ((), (), s32[]{:S(2)}) async-start(), calls=%async_computation.1 | async-start | bytes 4194304 | tf_op jit(solution)/shard_map/psum | solution.py:81
  149.2 101.9 %copy-start.1 = (f32[128,128]{1,0:T(8,128)S(1)}, f32[128,128]{1,0:T(8,128)}, u32[]{:S(2)}) copy-start(f32[128,128]{1,0:T(8,128)} %get-tuple-element.20) | copy-start | bytes 196612
  251.1 2.6 copy-start
Sparse Core Ops, SparseCore 0:
  9.7 32.9 all-reduce.4
  46.8 70.9 all-reduce.8
  149.3 101.6 all-reduce.6

commit v2 on v1

--- a/solution.py
+++ b/solution.py
@@ -1,3 +1,5 @@
+import functools
+
 import jax
 import jax.numpy as jnp
 from jax import lax
@@ -7,6 +9,8 @@
 
 PANEL = 128
 STRIP = 8
+LANES = 128
+MESH = pl.DeviceIdType.MESH
 
 
 def dot_exact(a, b, contract):
@@ -69,21 +73,270 @@
     return pl.pallas_call(factor_kernel, out_shape=(square, square), name="factorize")(gram, top)
 
 
-def on_device(matrix):
-    own = jnp.where(lax.axis_index("col") == 0, matrix[:, :PANEL], 0.0)
-    panel = lax.psum(own, "col")
+def everyone_ready(n_row, n_col):
+    row, col = lax.axis_index("row"), lax.axis_index("col")
+    barrier = pltpu.get_barrier_semaphore()
+    for d in range(1, n_row):
+        pl.semaphore_signal(barrier, inc=1, device_id={"row": lax.rem(row + d, n_row)}, device_id_type=MESH)
+    for d in range(1, n_col):
+        pl.semaphore_signal(barrier, inc=1, device_id={"col": lax.rem(col + d, n_col)}, device_id_type=MESH)
+    pl.semaphore_wait(barrier, n_row - 1 + max(n_col - 1, 0))
+
+
+def send(src, dst, send_sem, recv_sem, target):
+    return pltpu.make_async_remote_copy(
+        src_ref=src, dst_ref=dst, send_sem=send_sem, recv_sem=recv_sem, device_id=target, device_id_type=MESH
+    )
+
+
+def front_kernel(
+    n_row, n_col, matrix_ref, panel_out, gram_out, top_out,
+    panel, top, parts, arrived, whole, local_sem, panel_send, top_send, part_send, whole_send, share_send,
+    panel_recv, top_recv, part_recv, whole_recv, share_recv,
+):
+    row, col = lax.axis_index("row"), lax.axis_index("col")
+    piece = PANEL // n_row
+    everyone_ready(n_row, n_col)
+
+    @pl.when(col == 0)
+    def _():
+        fetch = pltpu.make_async_copy(matrix_ref.at[:, pl.ds(0, PANEL)], panel, local_sem.at[0])
+        fetch.start()
+        fetch.wait()
+        panel_copies = [
+            send(panel, panel, panel_send.at[c - 1], panel_recv.at[0], {"col": c}) for c in range(1, n_col)
+        ]
+
+        @pl.when(row == 0)
+        def _():
+            for r in range(1, n_row):
+                send(panel.at[pl.ds(0, PANEL)], top, top_send.at[r - 1], top_recv.at[0], {"row": r}).start()
+            own = pltpu.make_async_copy(panel.at[pl.ds(0, PANEL)], top, local_sem.at[1])
+            own.start()
+            own.wait()
+
+        local = dot_exact(panel[...], panel[...], ((0,), (0,)))
+        for q in range(n_row):
+            parts[q] = local[q * piece : (q + 1) * piece]
+        part_copies = []
+        for d in range(1, n_row):
+            q = lax.rem(row + d, n_row)
+            part_copies.append(
+                send(parts.at[q], arrived.at[d - 1], part_send.at[d - 1], part_recv.at[d - 1], {"row": q})
+            )
+            part_copies[-1].start()
+        for copy in panel_copies:
+            copy.start()
+        total = parts[row]
+        for d in range(1, n_row):
+            part_copies[d - 1].wait_recv()
+            total = total + arrived[d - 1]
+        whole[row] = total
+        whole_copies = []
+        for d in range(1, n_row):
+            q = lax.rem(row + d, n_row)
+            whole_copies.append(
+                send(whole.at[row], whole.at[row], whole_send.at[d - 1], whole_recv.at[d - 1], {"row": q})
+            )
+            whole_copies[-1].start()
+
+        @pl.when(row != 0)
+        def _():
+            send(top, top, top_send.at[0], top_recv.at[0], {"row": 0}).wait_recv()
+
+        for d in range(1, n_row):
+            q = lax.rem(row - d + n_row, n_row)
+            send(whole.at[q], whole.at[q], whole_send.at[d - 1], whole_recv.at[d - 1], {"row": q}).wait_recv()
+        shares = []
+        for c in range(1, n_col):
+            shares.append(send(top, top, share_send.at[2 * c - 2], share_recv.at[0], {"col": c}))
+            shares.append(send(whole, whole, share_send.at[2 * c - 1], share_recv.at[1], {"col": c}))
+        for copy in shares:
+            copy.start()
+
+        @pl.when(row == 0)
+        def _():
+            for r in range(1, n_row):
+                send(panel.at[pl.ds(0, PANEL)], top, top_send.at[r - 1], top_recv.at[0], {"row": r}).wait_send()
+
+        for copy in part_copies + panel_copies + whole_copies + shares:
+            copy.wait_send()
+
+    @pl.when(col != 0)
+    def _():
+        root = {"col": 0}
+        send(panel, panel, panel_send.at[0], panel_recv.at[0], root).wait_recv()
+        send(top, top, share_send.at[0], share_recv.at[0], root).wait_recv()
+        send(whole, whole, share_send.at[1], share_recv.at[1], root).wait_recv()
+
+    panel_out[...] = panel[...]
+    top_out[...] = top[...]
+    for q in range(n_row):
+        gram_out[q * piece : (q + 1) * piece] = whole[q]
+
+
+def front(matrix, n_row, n_col):
+    height = matrix.shape[0]
+    piece = PANEL // n_row
+    dma = pltpu.SemaphoreType.DMA
+    square = jax.ShapeDtypeStruct((PANEL, PANEL), jnp.float32)
+    return pl.pallas_call(
+        functools.partial(front_kernel, n_row, n_col),
+        out_shape=(jax.ShapeDtypeStruct((height, PANEL), jnp.float32), square, square),
+        in_specs=[pl.BlockSpec(memory_space=pl.ANY)],
+        out_specs=(pl.BlockSpec(memory_space=pltpu.VMEM),) * 3,
+        scratch_shapes=[
+            pltpu.VMEM((height, PANEL), jnp.float32),
+            pltpu.VMEM((PANEL, PANEL), jnp.float32),
+            pltpu.VMEM((n_row, piece, PANEL), jnp.float32),
+            pltpu.VMEM((n_row - 1, piece, PANEL), jnp.float32),
+            pltpu.VMEM((n_row, piece, PANEL), jnp.float32),
+            dma((2,)),
+            dma((n_col - 1,)),
+            dma((n_row - 1,)),
+            dma((n_row - 1,)),
+            dma((n_row - 1,)),
+            dma((2 * n_col - 2,)),
+            dma((1,)),
+            dma((1,)),
+            dma((n_row - 1,)),
+            dma((n_row - 1,)),
+            dma((2,)),
+        ],
+        compiler_params=pltpu.CompilerParams(collective_id=0, has_side_effects=True),
+        name="front",
+    )(matrix)
+
+
+def sum_kernel(
+    n_row, inner_n, chunks, part_ref, out_ref,
+    pair_in, half, far_in, hold, pair_send, far_send, done_send, back_send, pair_recv, far_recv, done_recv, back_recv,
+):
+    row = lax.axis_index("row")
+    outer_n = n_row // inner_n
+    outer, inner = row // inner_n, lax.rem(row, inner_n)
+    other = 1 - inner
+    partner = {"row": outer * inner_n + other}
+    span = outer_n * LANES
+    everyone_ready(n_row, 1)
+
+    def columns(k, i):
+        return pl.ds(pl.multiple_of((k * inner_n + i) * span, span), span)
+
+    def peer(d):
+        return lax.rem(outer + d, outer_n)
+
+    def pair(k):
+        return send(part_ref.at[:, columns(k, other)], pair_in.at[k], pair_send.at[k], pair_recv.at[k], partner)
+
+    def far(k, d):
+        q = peer(d)
+        return send(
+            half.at[k, q], far_in.at[k, d - 1], far_send.at[k, d - 1], far_recv.at[k, d - 1],
+            {"row": q * inner_n + inner},
+        )
+
+    def spot(k, o):
+        return pl.ds(pl.multiple_of((k * inner_n + inner) * span + o * LANES, LANES), LANES)
+
+    def done(k, d):
+        return send(
+            hold.at[:, spot(k, outer)], hold.at[:, spot(k, outer)], done_send.at[k, d - 1], done_recv.at[k, d - 1],
+            {"row": peer(d) * inner_n + inner},
+        )
+
+    def back(k):
+        return send(hold.at[:, columns(k, inner)], hold.at[:, columns(k, inner)], back_send.at[k], back_recv.at[k], partner)
+
+    def stage_far(k):
+        pair(k).wait_recv()
+        for o in range(outer_n):
+            place = pl.ds(pl.multiple_of((k * inner_n + inner) * span + o * LANES, LANES), LANES)
+            half[k, o] = part_ref[:, place] + pair_in[k, :, o * LANES : (o + 1) * LANES]
+        for d in range(1, outer_n):
+            far(k, d).start()
+
+    def stage_done(k):
+        total = half[k, outer]
+        for d in range(1, outer_n):
+            far(k, d).wait_recv()
+            total = total + far_in[k, d - 1]
+        hold[:, spot(k, outer)] = total
+        for d in range(1, outer_n):
+            done(k, d).start()
+
+    def stage_back(k):
+        for d in range(1, outer_n):
+            q = lax.rem(outer - d + outer_n, outer_n)
+            send(
+                hold.at[:, spot(k, q)], hold.at[:, spot(k, q)], done_send.at[k, d - 1], done_recv.at[k, d - 1],
+                {"row": q * inner_n + inner},
+            ).wait_recv()
+        back(k).start()
+
+    for k in range(chunks):
+        pair(k).start()
+    for step in range(chunks + 2):
+        if step < chunks:
+            stage_far(step)
+        if 0 <= step - 1 < chunks:
+            stage_done(step - 1)
+        if 0 <= step - 2 < chunks:
+            stage_back(step - 2)
+    for k in range(chunks):
+        mirror = hold.at[:, columns(k, other)]
+        send(mirror, mirror, back_send.at[k], back_recv.at[k], partner).wait_recv()
+    for k in range(chunks):
+        pair(k).wait_send()
+        back(k).wait_send()
+        for d in range(1, outer_n):
+            far(k, d).wait_send()
+            done(k, d).wait_send()
+    out_ref[...] = hold[...]
+
+
+def sum_rows(part, n_row):
+    width = part.shape[1]
+    inner_n = 2
+    outer_n = n_row // inner_n
+    chunks = width // (n_row * LANES)
+    span = outer_n * LANES
+    dma = pltpu.SemaphoreType.DMA
+    return pl.pallas_call(
+        functools.partial(sum_kernel, n_row, inner_n, chunks),
+        out_shape=jax.ShapeDtypeStruct(part.shape, jnp.float32),
+        in_specs=[pl.BlockSpec(memory_space=pltpu.VMEM)],
+        out_specs=pl.BlockSpec(memory_space=pltpu.VMEM),
+        scratch_shapes=[
+            pltpu.VMEM((chunks, PANEL, span), jnp.float32),
+            pltpu.VMEM((chunks, outer_n, PANEL, LANES), jnp.float32),
+            pltpu.VMEM((chunks, outer_n - 1, PANEL, LANES), jnp.float32),
+            pltpu.VMEM((PANEL, width), jnp.float32),
+            dma((chunks,)),
+            dma((chunks, outer_n - 1)),
+            dma((chunks, outer_n - 1)),
+            dma((chunks,)),
+            dma((chunks,)),
+            dma((chunks, outer_n - 1)),
+            dma((chunks, outer_n - 1)),
+            dma((chunks,)),
+        ],
+        compiler_params=pltpu.CompilerParams(collective_id=1, has_side_effects=True),
+        name="sum_rows",
+    )(part)
+
+
+def on_device(n_row, n_col, matrix):
+    panel, gram, top = front(matrix, n_row, n_col)
     first = lax.axis_index("row") == 0
-    gram_part = jnp.dot(panel.T, panel, precision=lax.Precision.HIGHEST)
-    gram, top = lax.psum((gram_part, jnp.where(first, panel[:PANEL], 0.0)), "row")
     factor, inverse = factorize(gram, top)
     shifted = panel.at[:PANEL].add(jnp.where(first, factor, 0.0))
     partial = lax.dot_general(shifted, matrix, (((0,), (0,)), ((), ())), precision=lax.Precision.HIGH)
-    summed = lax.psum(partial, "row")
+    summed = sum_rows(partial, n_row)
     coefficients = jnp.dot(inverse, summed, precision=lax.Precision.HIGH)
     return matrix - jnp.dot(shifted, coefficients, precision=lax.Precision.HIGH)
 
 
 def solution(mesh):
-    return jax.shard_map(
-        on_device, mesh=mesh, in_specs=(P("row", "col"),), out_specs=P("row", "col"), check_vma=False
-    )
+    body = functools.partial(on_device, mesh.shape["row"], mesh.shape["col"])
+    return jax.shard_map(body, mesh=mesh, in_specs=(P("row", "col"),), out_specs=P("row", "col"), check_vma=False)

time: 273 us -> 138 us (0.51)
  waiting for transfers between devices: 207 us -> 0 us
  Pallas kernels: 20.2 us -> 113 us
  between operations: 13.1 us -> 0.05 us
  other arithmetic: 4.7 us -> 1.46 us
    psum x3 -> x0, waiting for transfers between devices: 207 us -> none  [the longest x1 102 us: on_device(): summed = lax.psum(partial, 'row')]
    pallas_call x0 -> x2, Pallas kernels: none -> 93.1 us  [the longest x1 71 us: sum_rows(): pl.pallas_call(functools.partial(sum_kernel, n_row, inner_n, chunks), out...]
    select_n x2 -> x0, other arithmetic: 3.24 us -> none  [the longest x1 1.77 us: on_device(): own = jnp.where(lax.axis_index('col') == 0, matrix[:, :PANEL], 0.0)]
  transfers between devices with their start and end apart: 3 -> 0, of which waited for: 3 -> 0; matrix products, arithmetic and copies ran while one was open for 0% -> 0% of each run, Pallas kernels for 0% -> 0%
where the time goes in v2:
time: 138 us
  Pallas kernels  113 us (82%)
  matrix products  23.1 us (17%)
  other arithmetic  1.46 us (1%)
    pallas_call x1, Pallas kernels, sum_rows(): pl.pallas_call(functools.partial(sum_kernel, n_row, inner_n, chunks), out...  71 us
    pallas_call x1, Pallas kernels, front(): pl.pallas_call(functools.partial(front_kernel, n_row, n_col), out_shape=(...  22.1 us
    pallas_call x1, Pallas kernels, factorize(): pl.pallas_call(factor_kernel, out_shape=(square, square), name='factorize')  20.2 us
    dot_general x1, matrix products, on_device(): return matrix - jnp.dot(shifted, coefficients, precision=lax.Precision.HIGH)  10.9 us
    dot_general x1, matrix products, on_device(): lax.dot_general(shifted, matrix, (((0,), (0,)), ((), ())), precision=lax....  9.62 us

profile of v2, /device:TPU:10, one launch (start us, length us, event | category | flops | bytes accessed | tf_op | source)
XLA Modules:
  0.0 137.9 jit_solution(926573122380532385)
XLA Ops:
  0.0 22.1 %front.1 = (f32[768,128]{1,0:T(8,128)}, f32[128,128]{1,0:T(8,128)}, f32[128,128]{1,0:T(8,128)}) custom-call(f32[768,4096]{1,0:T(8,128)} %matrix_ref.1), custom_call_target="tpu_custom_call" | custom-call | tf_op jit(solution)/shard_map/front/pallas_call | solution.py:183
  22.1 20.2 %factorize.1 = (f32[128,128]{1,0:T(8,128)}, f32[128,128]{1,0:T(8,128)}) custom-call(f32[128,128]{1,0:T(8,128)} %get-tuple-element.23.gram_ref, f32[128,128]{1,0:T(8,128)} %get-tuple-element.24.top_ref), custom_call_target="tpu_custom_call" | custom-call | tf_op jit(solution)/shard_map/factorize/pallas_call | solution.py:73
  42.3 1.5 %add_dynamic-update-slice_fusion = f32[768,128]{1,0:T(8,128)} fusion(f32[768,128]{1,0:T(8,128)} %get-tuple-element.22, f32[128,128]{1,0:T(8,128)} %get-tuple-element.25, pred[]{:T(512)S(6)} %eq.3), kind=kLoop, calls=%fused_computation.1 | loop fusion | flops 32768 | bytes 196609 | tf_op jit(solution)/shard_map/scatter-add | solution.py:333
  43.8 9.6 %fusion.part_ref = f32[128,4096]{1,0:T(8,128)} fusion(f32[768,128]{1,0:T(8,128)} %add_dynamic-update-slice_fusion, f32[768,4096]{1,0:T(8,128)} %matrix_ref.1), kind=kOutput, calls=%fused_computation.2 | convolution fusion | flops 2415919104 | bytes 15073280 | tf_op jit(solution)/shard_map/dot_general | solution.py:334
  53.4 0.0 copy-start.1
  53.4 71.0 %sum_rows.1 = f32[128,4096]{1,0:T(8,128)} custom-call(f32[128,4096]{1,0:T(8,128)} %fusion.part_ref), custom_call_target="tpu_custom_call" | custom-call | tf_op jit(solution)/shard_map/sum_rows/pallas_call | solution.py:305
  124.4 0.0 copy-done.1
  124.4 0.0 copy-start
  124.4 2.6 %fusion.1 = f32[128,4096]{1,0:T(8,128)S(1)} fusion(f32[128,128]{1,0:T(8,128)S(1)} %copy-done.1, f32[128,4096]{1,0:T(8,128)} %sum_rows.1), kind=kOutput, calls=%fused_computation.3 | convolution fusion | flops 402653184 | bytes 4259840 | tf_op jit(solution)/shard_map/dot_general | solution.py:336
  127.0 0.0 copy-done
  127.0 10.9 %convolution_subtract_fusion = f32[768,4096]{1,0:T(8,128)} fusion(f32[768,4096]{1,0:T(8,128)} %matrix_ref.1, f32[768,128]{1,0:T(8,128)S(1)} %copy-done, f32[128,4096]{1,0:T(8,128)S(1)} %fusion.1), kind=kOutput, calls=%fused_computation | convolution fusion | flops 2419064832 | bytes 27656192 | tf_op jit(solution)/shard_map/dot_general | solution.py:337
Async XLA Ops:
  53.4 71.0 %copy-start.1 = (f32[128,128]{1,0:T(8,128)S(1)}, f32[128,128]{1,0:T(8,128)}, u32[]{:S(2)}) copy-start(f32[128,128]{1,0:T(8,128)} %get-tuple-element.26) | copy-start | bytes 196612
  124.4 2.6 %copy-start = (f32[768,128]{1,0:T(8,128)S(1)}, f32[768,128]{1,0:T(8,128)}, u32[]{:S(2)}) copy-start(f32[768,128]{1,0:T(8,128)} %add_dynamic-update-slice_fusion) | copy-start | bytes 1179652

commit v3 on v2

--- a/solution.py
+++ b/solution.py
@@ -19,7 +19,7 @@
     )
 
 
-def factor_values(gram, top):
+def factor_values(gram, top, between=lambda strip: None):
     strips = PANEL // STRIP
     rows = lax.broadcasted_iota(jnp.int32, (STRIP, 1), 0)
     eye = (
@@ -29,6 +29,7 @@
     work = jnp.concatenate([top, jnp.zeros_like(top)], axis=1)
     factor_rows = []
     for strip in range(strips):
+        between(strip)
         at = strip * STRIP
         panel = chol[:STRIP]
         scale = jnp.ones((STRIP, 1), jnp.float32)
@@ -62,17 +63,6 @@
     return jnp.concatenate(factor_rows, axis=0), work[:, PANEL:]
 
 
-def factor_kernel(gram_ref, top_ref, factor_ref, inverse_ref):
-    factor, inverse = factor_values(gram_ref[...], top_ref[...])
-    factor_ref[...] = factor
-    inverse_ref[...] = inverse
-
-
-def factorize(gram, top):
-    square = jax.ShapeDtypeStruct((PANEL, PANEL), jnp.float32)
-    return pl.pallas_call(factor_kernel, out_shape=(square, square), name="factorize")(gram, top)
-
-
 def everyone_ready(n_row, n_col):
     row, col = lax.axis_index("row"), lax.axis_index("col")
     barrier = pltpu.get_barrier_semaphore()
@@ -89,20 +79,60 @@
     )
 
 
-def front_kernel(
-    n_row, n_col, matrix_ref, panel_out, gram_out, top_out,
-    panel, top, parts, arrived, whole, local_sem, panel_send, top_send, part_send, whole_send, share_send,
-    panel_recv, top_recv, part_recv, whole_recv, share_recv,
+def split(x):
+    high = x.astype(jnp.bfloat16)
+    return high, (x - high.astype(jnp.float32)).astype(jnp.bfloat16)
+
+
+def step_kernel(
+    n_row, n_col, inner_n, chunks, matrix_ref, shifted_out, hold,
+    block, partial, stacked, pair_in, half, far_in, top_in, panel, top, parts, arrived, whole,
+    local_sem, block_sem, own_sem,
+    panel_send, top_send, part_send, whole_send, share_send, scatter_send,
+    panel_recv, top_recv, part_recv, whole_recv, share_recv, scatter_recv,
+    pair_send, far_send, done_send, back_send, pair_recv, far_recv, done_recv, back_recv,
 ):
     row, col = lax.axis_index("row"), lax.axis_index("col")
     piece = PANEL // n_row
+    outer_n = n_row // inner_n
+    outer, inner = row // inner_n, lax.rem(row, inner_n)
+    other = 1 - inner
+    partner = {"row": outer * inner_n + other}
+    span = outer_n * LANES
     everyone_ready(n_row, n_col)
+
+    def load(k):
+        place = pl.ds(k * inner_n * span, inner_n * span)
+        return pltpu.make_async_copy(matrix_ref.at[:, place], block.at[:, place], block_sem.at[k])
+
+    def scatter(k, r):
+        place = pl.ds((k * inner_n + r % inner_n) * span + r // inner_n * LANES, LANES)
+        return send(
+            matrix_ref.at[pl.ds(0, PANEL), place], top_in.at[k],
+            scatter_send.at[k, r - 1], scatter_recv.at[k], {"row": r},
+        )
+
+    def keep(k):
+        place = pl.ds(k * inner_n * span, LANES)
+        return pltpu.make_async_copy(matrix_ref.at[pl.ds(0, PANEL), place], top_in.at[k], own_sem.at[k])
+
+    def start_scatter():
+        for k in range(chunks):
+            for r in range(1, n_row):
+                scatter(k, r).start()
+            keep(k).start()
+
+    @pl.when((row == 0) & (col != 0))
+    def _():
+        start_scatter()
 
     @pl.when(col == 0)
     def _():
         fetch = pltpu.make_async_copy(matrix_ref.at[:, pl.ds(0, PANEL)], panel, local_sem.at[0])
         fetch.start()
         fetch.wait()
+        for k in range(chunks):
+            load(k).start()
         panel_copies = [
             send(panel, panel, panel_send.at[c - 1], panel_recv.at[0], {"col": c}) for c in range(1, n_col)
         ]
@@ -164,61 +194,16 @@
 
     @pl.when(col != 0)
     def _():
+        for k in range(chunks):
+            load(k).start()
         root = {"col": 0}
         send(panel, panel, panel_send.at[0], panel_recv.at[0], root).wait_recv()
         send(top, top, share_send.at[0], share_recv.at[0], root).wait_recv()
         send(whole, whole, share_send.at[1], share_recv.at[1], root).wait_recv()
 
-    panel_out[...] = panel[...]
-    top_out[...] = top[...]
-    for q in range(n_row):
-        gram_out[q * piece : (q + 1) * piece] = whole[q]
-
-
-def front(matrix, n_row, n_col):
-    height = matrix.shape[0]
-    piece = PANEL // n_row
-    dma = pltpu.SemaphoreType.DMA
-    square = jax.ShapeDtypeStruct((PANEL, PANEL), jnp.float32)
-    return pl.pallas_call(
-        functools.partial(front_kernel, n_row, n_col),
-        out_shape=(jax.ShapeDtypeStruct((height, PANEL), jnp.float32), square, square),
-        in_specs=[pl.BlockSpec(memory_space=pl.ANY)],
-        out_specs=(pl.BlockSpec(memory_space=pltpu.VMEM),) * 3,
-        scratch_shapes=[
-            pltpu.VMEM((height, PANEL), jnp.float32),
-            pltpu.VMEM((PANEL, PANEL), jnp.float32),
-            pltpu.VMEM((n_row, piece, PANEL), jnp.float32),
-            pltpu.VMEM((n_row - 1, piece, PANEL), jnp.float32),
-            pltpu.VMEM((n_row, piece, PANEL), jnp.float32),
-            dma((2,)),
-            dma((n_col - 1,)),
-            dma((n_row - 1,)),
-            dma((n_row - 1,)),
-            dma((n_row - 1,)),
-            dma((2 * n_col - 2,)),
-            dma((1,)),
-            dma((1,)),
-            dma((n_row - 1,)),
-            dma((n_row - 1,)),
-            dma((2,)),
-        ],
-        compiler_params=pltpu.CompilerParams(collective_id=0, has_side_effects=True),
-        name="front",
-    )(matrix)
-
-
-def sum_kernel(
-    n_row, inner_n, chunks, part_ref, out_ref,
-    pair_in, half, far_in, hold, pair_send, far_send, done_send, back_send, pair_recv, far_recv, done_recv, back_recv,
-):
-    row = lax.axis_index("row")
-    outer_n = n_row // inner_n
-    outer, inner = row // inner_n, lax.rem(row, inner_n)
-    other = 1 - inner
-    partner = {"row": outer * inner_n + other}
-    span = outer_n * LANES
-    everyone_ready(n_row, 1)
+    @pl.when((row == 0) & (col == 0))
+    def _():
+        start_scatter()
 
     def columns(k, i):
         return pl.ds(pl.multiple_of((k * inner_n + i) * span, span), span)
@@ -227,7 +212,7 @@
         return lax.rem(outer + d, outer_n)
 
     def pair(k):
-        return send(part_ref.at[:, columns(k, other)], pair_in.at[k], pair_send.at[k], pair_recv.at[k], partner)
+        return send(partial.at[:, columns(k, other)], pair_in.at[k], pair_send.at[k], pair_recv.at[k], partner)
 
     def far(k, d):
         q = peer(d)
@@ -248,20 +233,36 @@
     def back(k):
         return send(hold.at[:, columns(k, inner)], hold.at[:, columns(k, inner)], back_send.at[k], back_recv.at[k], partner)
 
+    def multiply(k, i):
+        place = columns(k, i)
+        high, low = split(block[:, place])
+        both = jnp.dot(stacked[...], high, preferred_element_type=jnp.float32)
+        rest = jnp.dot(stacked[:PANEL], low, preferred_element_type=jnp.float32)
+        partial[:, place] = both[:PANEL] + both[PANEL:] + rest
+
     def stage_far(k):
         pair(k).wait_recv()
         for o in range(outer_n):
-            place = pl.ds(pl.multiple_of((k * inner_n + inner) * span + o * LANES, LANES), LANES)
-            half[k, o] = part_ref[:, place] + pair_in[k, :, o * LANES : (o + 1) * LANES]
+            half[k, o] = partial[:, spot(k, o)] + pair_in[k, :, o * LANES : (o + 1) * LANES]
         for d in range(1, outer_n):
             far(k, d).start()
 
-    def stage_done(k):
+    def stage_done(k, factor, inverse):
         total = half[k, outer]
         for d in range(1, outer_n):
             far(k, d).wait_recv()
             total = total + far_in[k, d - 1]
-        hold[:, spot(k, outer)] = total
+
+        @pl.when(row == 0)
+        def _():
+            keep(k).wait()
+
+        @pl.when(row != 0)
+        def _():
+            send(top_in.at[k], top_in.at[k], scatter_send.at[k, 0], scatter_recv.at[k], {"row": 0}).wait_recv()
+
+        total = total + dot_exact(factor, top_in[k], ((0,), (0,)))
+        hold[:, spot(k, outer)] = dot_exact(inverse, total, ((1,), (0,)))
         for d in range(1, outer_n):
             done(k, d).start()
 
@@ -275,14 +276,41 @@
         back(k).start()
 
     for k in range(chunks):
-        pair(k).start()
+        load(k).wait()
+    high, low = split(jnp.transpose(panel[...]))
+    stacked[:PANEL] = high
+    stacked[PANEL:] = low
+    gram = jnp.concatenate([whole[q] for q in range(n_row)], axis=0)
+
+    def between(strip):
+        if strip < chunks:
+            multiply(strip, other)
+            pair(strip).start()
+        elif strip < 2 * chunks:
+            multiply(strip - chunks, inner)
+        elif strip >= 2 * chunks + 2 and strip % 2 == 0 and (strip - 2 * chunks - 2) // 2 < chunks - 1:
+            stage_far((strip - 2 * chunks - 2) // 2)
+
+    ready = max(0, min(chunks - 1, (PANEL // STRIP - 2 * chunks - 1) // 2))
+    factor, inverse = factor_values(gram, top[...], between)
     for step in range(chunks + 2):
-        if step < chunks:
-            stage_far(step)
-        if 0 <= step - 1 < chunks:
-            stage_done(step - 1)
+        if step < ready:
+            stage_done(step, factor, inverse)
+        if ready + step < chunks:
+            stage_far(ready + step)
+        if ready <= step < chunks:
+            stage_done(step, factor, inverse)
         if 0 <= step - 2 < chunks:
             stage_back(step - 2)
+    shifted_out[...] = panel[...]
+
+    @pl.when(row == 0)
+    def _():
+        shifted_out[:PANEL] = panel[:PANEL] + factor
+        for k in range(chunks):
+            for r in range(1, n_row):
+                scatter(k, r).wait_send()
+
     for k in range(chunks):
         mirror = hold.at[:, columns(k, other)]
         send(mirror, mirror, back_send.at[k], back_recv.at[k], partner).wait_recv()
@@ -292,26 +320,50 @@
         for d in range(1, outer_n):
             far(k, d).wait_send()
             done(k, d).wait_send()
-    out_ref[...] = hold[...]
-
-
-def sum_rows(part, n_row):
-    width = part.shape[1]
+
+
+def whole_step(matrix, n_row, n_col):
+    height, width = matrix.shape
+    piece = PANEL // n_row
     inner_n = 2
     outer_n = n_row // inner_n
     chunks = width // (n_row * LANES)
     span = outer_n * LANES
     dma = pltpu.SemaphoreType.DMA
+    f32 = jnp.float32
     return pl.pallas_call(
-        functools.partial(sum_kernel, n_row, inner_n, chunks),
-        out_shape=jax.ShapeDtypeStruct(part.shape, jnp.float32),
-        in_specs=[pl.BlockSpec(memory_space=pltpu.VMEM)],
-        out_specs=pl.BlockSpec(memory_space=pltpu.VMEM),
+        functools.partial(step_kernel, n_row, n_col, inner_n, chunks),
+        out_shape=(jax.ShapeDtypeStruct((height, PANEL), f32), jax.ShapeDtypeStruct((PANEL, width), f32)),
+        in_specs=[pl.BlockSpec(memory_space=pl.ANY)],
+        out_specs=(pl.BlockSpec(memory_space=pltpu.VMEM),) * 2,
         scratch_shapes=[
-            pltpu.VMEM((chunks, PANEL, span), jnp.float32),
-            pltpu.VMEM((chunks, outer_n, PANEL, LANES), jnp.float32),
-            pltpu.VMEM((chunks, outer_n - 1, PANEL, LANES), jnp.float32),
-            pltpu.VMEM((PANEL, width), jnp.float32),
+            pltpu.VMEM((height, width), f32),
+            pltpu.VMEM((PANEL, width), f32),
+            pltpu.VMEM((2 * PANEL, height), jnp.bfloat16),
+            pltpu.VMEM((chunks, PANEL, span), f32),
+            pltpu.VMEM((chunks, outer_n, PANEL, LANES), f32),
+            pltpu.VMEM((chunks, outer_n - 1, PANEL, LANES), f32),
+            pltpu.VMEM((chunks, PANEL, LANES), f32),
+            pltpu.VMEM((height, PANEL), f32),
+            pltpu.VMEM((PANEL, PANEL), f32),
+            pltpu.VMEM((n_row, piece, PANEL), f32),
+            pltpu.VMEM((n_row - 1, piece, PANEL), f32),
+            pltpu.VMEM((n_row, piece, PANEL), f32),
+            dma((2,)),
+            dma((chunks,)),
+            dma((chunks,)),
+            dma((n_col - 1,)),
+            dma((n_row - 1,)),
+            dma((n_row - 1,)),
+            dma((n_row - 1,)),
+            dma((2 * n_col - 2,)),
+            dma((chunks, n_row - 1)),
+            dma((1,)),
+            dma((1,)),
+            dma((n_row - 1,)),
+            dma((n_row - 1,)),
+            dma((2,)),
+            dma((chunks,)),
             dma((chunks,)),
             dma((chunks, outer_n - 1)),
             dma((chunks, outer_n - 1)),
@@ -321,19 +373,15 @@
             dma((chunks, outer_n - 1)),
             dma((chunks,)),
         ],
-        compiler_params=pltpu.CompilerParams(collective_id=1, has_side_effects=True),
-        name="sum_rows",
-    )(part)
+        compiler_params=pltpu.CompilerParams(
+            collective_id=0, has_side_effects=True, vmem_limit_bytes=48 * 1024 * 1024
+        ),
+        name="whole_step",
+    )(matrix)
 
 
 def on_device(n_row, n_col, matrix):
-    panel, gram, top = front(matrix, n_row, n_col)
-    first = lax.axis_index("row") == 0
-    factor, inverse = factorize(gram, top)
-    shifted = panel.at[:PANEL].add(jnp.where(first, factor, 0.0))
-    partial = lax.dot_general(shifted, matrix, (((0,), (0,)), ((), ())), precision=lax.Precision.HIGH)
-    summed = sum_rows(partial, n_row)
-    coefficients = jnp.dot(inverse, summed, precision=lax.Precision.HIGH)
+    shifted, coefficients = whole_step(matrix, n_row, n_col)
     return matrix - jnp.dot(shifted, coefficients, precision=lax.Precision.HIGH)
 
 

time: 138 us -> 110 us (0.80)
  the two profiles are of different devices: /device:TPU:10 before, /device:TPU:28 now
where the time goes in v3:
time: 110 us
  Pallas kernels  102 us (93%)
  matrix products  7.96 us (7%)
    pallas_call x1, Pallas kernels, whole_step(): pl.pallas_call(functools.partial(step_kernel, n_row, n_col, inner_n, chun...  102 us
    dot_general x1, matrix products, on_device(): return matrix - jnp.dot(shifted, coefficients, precision=lax.Precision.HIGH)  7.96 us

profile of v3, /device:TPU:28, one launch (start us, length us, event | category | flops | bytes accessed | tf_op | source)
XLA Modules:
  0.0 110.3 jit_solution(11634395912936720747)
XLA Ops:
  0.0 0.0 copy-start
  0.0 102.3 %whole_step.1 = (f32[768,128]{1,0:T(8,128)S(1)}, f32[128,4096]{1,0:T(8,128)S(1)}) custom-call(f32[768,4096]{1,0:T(8,128)} %matrix_ref.1), custom_call_target="tpu_custom_call" | custom-call | tf_op jit(solution)/shard_map/whole_step/pallas_call | solution.py:334
  102.3 0.0 copy-done
  102.3 8.0 %convolution_subtract_fusion = f32[768,4096]{1,0:T(8,128)} fusion(f32[768,4096]{1,0:T(8,128)S(1)} %copy-done, f32[768,128]{1,0:T(8,128)S(1)} %get-tuple-element.7, f32[128,4096]{1,0:T(8,128)S(1)} %get-tuple-element.8), kind=kOutput, calls=%fused_computation | convolution fusion | flops 2419064832 | bytes 27656192 | tf_op jit(solution)/shard_map/dot_general | solution.py:385
Async XLA Ops:
  0.0 102.3 %copy-start = (f32[768,4096]{1,0:T(8,128)S(1)}, f32[768,4096]{1,0:T(8,128)}, u32[]{:S(2)}) copy-start(f32[768,4096]{1,0:T(8,128)} %matrix_ref.1) | copy-start | bytes 37748740

commit v4 on v3

--- a/solution.py
+++ b/solution.py
@@ -28,38 +28,45 @@
     chol = jnp.concatenate([gram, eye], axis=1)
     work = jnp.concatenate([top, jnp.zeros_like(top)], axis=1)
     factor_rows = []
-    for strip in range(strips):
-        between(strip)
-        at = strip * STRIP
-        panel = chol[:STRIP]
-        scale = jnp.ones((STRIP, 1), jnp.float32)
+    lanes = lax.broadcasted_iota(jnp.int32, (STRIP, 2 * PANEL), 1)
+    previous = None
+    for strip in range(strips + 1):
+        at, back = strip * STRIP, (strip - 1) * STRIP
+        if strip < strips:
+            between(strip)
+            panel = chol[:STRIP]
+            scale = jnp.ones((STRIP, 1), jnp.float32)
+        if strip > 0:
+            inner = work[back : back + STRIP] + previous
+            aside = work[:, back : back + STRIP]
         for j in range(STRIP):
-            column = panel[:, at + j : at + j + 1]
-            pivot = column[j : j + 1]
-            multiplier = jnp.where(rows > j, column / pivot, 0.0)
-            scale = jnp.where(rows == j, lax.rsqrt(pivot), scale)
-            panel = panel - multiplier * panel[j : j + 1]
-        panel = panel * scale
-        lanes = lax.broadcasted_iota(jnp.int32, (STRIP, 2 * PANEL), 1)
-        panel = jnp.where(lanes >= at + rows, panel, 0.0)
-        factor_rows.append(panel[:, :PANEL])
-        if strip < strips - 1:
-            below = panel[:, at + STRIP : PANEL]
-            chol = chol[STRIP:] - dot_exact(below, panel, ((0,), (0,)))
-
-        inner = work[at : at + STRIP] + panel
-        for j in range(STRIP):
-            column = inner[:, at + j : at + j + 1]
-            pivot_row = inner[j : j + 1] / column[j : j + 1]
-            inner = jnp.where(rows == j, pivot_row, inner - column * pivot_row)
-        update = dot_exact(work[:, at : at + STRIP], inner, ((1,), (0,)))
-        pieces = []
-        if at > 0:
-            pieces.append(work[:at] - update[:at])
-        pieces.append(inner)
-        if strip < strips - 1:
-            pieces.append(work[at + STRIP :] - update[at + STRIP :])
-        work = jnp.concatenate(pieces, axis=0)
+            if strip < strips:
+                column = panel[:, at + j : at + j + 1]
+                pivot = column[j : j + 1]
+                multiplier = jnp.where(rows > j, column / pivot, 0.0)
+            if strip > 0:
+                inner_column = inner[:, back + j : back + j + 1]
+                pivot_row = inner[j : j + 1] / inner_column[j : j + 1]
+            if strip < strips:
+                scale = jnp.where(rows == j, lax.rsqrt(pivot), scale)
+                panel = panel - multiplier * panel[j : j + 1]
+            if strip > 0:
+                inner = jnp.where(rows == j, pivot_row, inner - inner_column * pivot_row)
+        if strip < strips:
+            panel = jnp.where(lanes >= at + rows, panel * scale, 0.0)
+            factor_rows.append(panel[:, :PANEL])
+            if strip < strips - 1:
+                chol = chol[STRIP:] - dot_exact(panel[:, at + STRIP : PANEL], panel, ((0,), (0,)))
+        if strip > 0:
+            update = dot_exact(aside, inner, ((1,), (0,)))
+            pieces = []
+            if back > 0:
+                pieces.append(work[:back] - update[:back])
+            pieces.append(inner)
+            if strip < strips:
+                pieces.append(work[at:] - update[at:])
+            work = jnp.concatenate(pieces, axis=0)
+        previous = panel
     return jnp.concatenate(factor_rows, axis=0), work[:, PANEL:]
 
 

time: 110 us -> 109 us (level)
  the two profiles are of different devices: /device:TPU:28 before, /device:TPU:10 now
where the time goes in v4:
time: 109 us
  Pallas kernels  101 us (93%)
  matrix products  7.95 us (7%)
    pallas_call x1, Pallas kernels, whole_step(): pl.pallas_call(functools.partial(step_kernel, n_row, n_col, inner_n, chun...  101 us
    dot_general x1, matrix products, on_device(): return matrix - jnp.dot(shifted, coefficients, precision=lax.Precision.HIGH)  7.95 us

profile of v4, /device:TPU:10, one launch (start us, length us, event | category | flops | bytes accessed | tf_op | source)
XLA Modules:
  0.0 109.3 jit_solution(9456551447335666044)
XLA Ops:
  0.0 0.0 copy-start
  0.0 101.3 %whole_step.1 = (f32[768,128]{1,0:T(8,128)S(1)}, f32[128,4096]{1,0:T(8,128)S(1)}) custom-call(f32[768,4096]{1,0:T(8,128)} %matrix_ref.1), custom_call_target="tpu_custom_call" | custom-call | tf_op jit(solution)/shard_map/whole_step/pallas_call | solution.py:341
  101.3 0.0 copy-done
  101.3 8.0 %convolution_subtract_fusion = f32[768,4096]{1,0:T(8,128)} fusion(f32[768,4096]{1,0:T(8,128)S(1)} %copy-done, f32[768,128]{1,0:T(8,128)S(1)} %get-tuple-element.7, f32[128,4096]{1,0:T(8,128)S(1)} %get-tuple-element.8), kind=kOutput, calls=%fused_computation | convolution fusion | flops 2419064832 | bytes 27656192 | tf_op jit(solution)/shard_map/dot_general | solution.py:392
Async XLA Ops:
  0.0 101.3 %copy-start = (f32[768,4096]{1,0:T(8,128)S(1)}, f32[768,4096]{1,0:T(8,128)}, u32[]{:S(2)}) copy-start(f32[768,4096]{1,0:T(8,128)} %matrix_ref.1) | copy-start | bytes 37748740

commit v5 on v4

--- a/solution.py
+++ b/solution.py
@@ -129,6 +129,48 @@
                 scatter(k, r).start()
             keep(k).start()
 
+    def columns(k, i):
+        return pl.ds(pl.multiple_of((k * inner_n + i) * span, span), span)
+
+    def peer(d):
+        return lax.rem(outer + d, outer_n)
+
+    def pair(k):
+        return send(partial.at[:, columns(k, other)], pair_in.at[k], pair_send.at[k], pair_recv.at[k], partner)
+
+    def far(k, d):
+        q = peer(d)
+        return send(
+            half.at[k, q], far_in.at[k, d - 1], far_send.at[k, d - 1], far_recv.at[k, d - 1],
+            {"row": q * inner_n + inner},
+        )
+
+    def spot(k, o):
+        return pl.ds(pl.multiple_of((k * inner_n + inner) * span + o * LANES, LANES), LANES)
+
+    def done(k, d):
+        return send(
+            hold.at[:, spot(k, outer)], hold.at[:, spot(k, outer)], done_send.at[k, d - 1], done_recv.at[k, d - 1],
+            {"row": peer(d) * inner_n + inner},
+        )
+
+    def back(k):
+        return send(hold.at[:, columns(k, inner)], hold.at[:, columns(k, inner)], back_send.at[k], back_recv.at[k], partner)
+
+    def multiply(k, i):
+        place = columns(k, i)
+        high, low = split(block[:, place])
+        both = jnp.dot(stacked[...], high, preferred_element_type=jnp.float32)
+        rest = jnp.dot(stacked[:PANEL], low, preferred_element_type=jnp.float32)
+        partial[:, place] = both[:PANEL] + both[PANEL:] + rest
+
+    def prepare():
+        for k in range(chunks):
+            load(k).wait()
+        high, low = split(jnp.transpose(panel[...]))
+        stacked[:PANEL] = high
+        stacked[PANEL:] = low
+
     @pl.when((row == 0) & (col != 0))
     def _():
         start_scatter()
@@ -164,6 +206,10 @@
             part_copies[-1].start()
         for copy in panel_copies:
             copy.start()
+        prepare()
+        early = min(2, chunks)
+        for k in range(early):
+            multiply(k, other)
         total = parts[row]
         for d in range(1, n_row):
             part_copies[d - 1].wait_recv()
@@ -176,6 +222,14 @@
                 send(whole.at[row], whole.at[row], whole_send.at[d - 1], whole_recv.at[d - 1], {"row": q})
             )
             whole_copies[-1].start()
+        for k in range(early, chunks):
+            multiply(k, other)
+        for k in range(chunks):
+            pair(k).start()
+
+        @pl.when(row == 0)
+        def _():
+            start_scatter()
 
         @pl.when(row != 0)
         def _():
@@ -205,47 +259,12 @@
             load(k).start()
         root = {"col": 0}
         send(panel, panel, panel_send.at[0], panel_recv.at[0], root).wait_recv()
+        prepare()
+        for k in range(chunks):
+            multiply(k, other)
+            pair(k).start()
         send(top, top, share_send.at[0], share_recv.at[0], root).wait_recv()
         send(whole, whole, share_send.at[1], share_recv.at[1], root).wait_recv()
-
-    @pl.when((row == 0) & (col == 0))
-    def _():
-        start_scatter()
-
-    def columns(k, i):
-        return pl.ds(pl.multiple_of((k * inner_n + i) * span, span), span)
-
-    def peer(d):
-        return lax.rem(outer + d, outer_n)
-
-    def pair(k):
-        return send(partial.at[:, columns(k, other)], pair_in.at[k], pair_send.at[k], pair_recv.at[k], partner)
-
-    def far(k, d):
-        q = peer(d)
-        return send(
-            half.at[k, q], far_in.at[k, d - 1], far_send.at[k, d - 1], far_recv.at[k, d - 1],
-            {"row": q * inner_n + inner},
-        )
-
-    def spot(k, o):
-        return pl.ds(pl.multiple_of((k * inner_n + inner) * span + o * LANES, LANES), LANES)
-
-    def done(k, d):
-        return send(
-            hold.at[:, spot(k, outer)], hold.at[:, spot(k, outer)], done_send.at[k, d - 1], done_recv.at[k, d - 1],
-            {"row": peer(d) * inner_n + inner},
-        )
-
-    def back(k):
-        return send(hold.at[:, columns(k, inner)], hold.at[:, columns(k, inner)], back_send.at[k], back_recv.at[k], partner)
-
-    def multiply(k, i):
-        place = columns(k, i)
-        high, low = split(block[:, place])
-        both = jnp.dot(stacked[...], high, preferred_element_type=jnp.float32)
-        rest = jnp.dot(stacked[:PANEL], low, preferred_element_type=jnp.float32)
-        partial[:, place] = both[:PANEL] + both[PANEL:] + rest
 
     def stage_far(k):
         pair(k).wait_recv()
@@ -282,23 +301,16 @@
             ).wait_recv()
         back(k).start()
 
-    for k in range(chunks):
-        load(k).wait()
-    high, low = split(jnp.transpose(panel[...]))
-    stacked[:PANEL] = high
-    stacked[PANEL:] = low
     gram = jnp.concatenate([whole[q] for q in range(n_row)], axis=0)
 
     def between(strip):
         if strip < chunks:
-            multiply(strip, other)
-            pair(strip).start()
-        elif strip < 2 * chunks:
-            multiply(strip - chunks, inner)
-        elif strip >= 2 * chunks + 2 and strip % 2 == 0 and (strip - 2 * chunks - 2) // 2 < chunks - 1:
-            stage_far((strip - 2 * chunks - 2) // 2)
-
-    ready = max(0, min(chunks - 1, (PANEL // STRIP - 2 * chunks - 1) // 2))
+            multiply(strip, inner)
+        elif strip >= first_far and (strip - first_far) % 3 == 0 and (strip - first_far) // 3 < ready:
+            stage_far((strip - first_far) // 3)
+
+    first_far = 2 * chunks
+    ready = max(0, min(chunks - 1, (PANEL // STRIP - first_far + 2) // 3))
     factor, inverse = factor_values(gram, top[...], between)
     for step in range(chunks + 2):
         if step < ready:

time: 109 us -> 108 us (level)
  the two profiles are of different devices: /device:TPU:10 before, /device:TPU:28 now
where the time goes in v5:
time: 108 us
  Pallas kernels  100 us (93%)
  matrix products  7.96 us (7%)
    pallas_call x1, Pallas kernels, whole_step(): pl.pallas_call(functools.partial(step_kernel, n_row, n_col, inner_n, chun...  100 us
    dot_general x1, matrix products, on_device(): return matrix - jnp.dot(shifted, coefficients, precision=lax.Precision.HIGH)  7.96 us

profile of v5, /device:TPU:28, one launch (start us, length us, event | category | flops | bytes accessed | tf_op | source)
XLA Modules:
  0.0 108.0 jit_solution(14633575635359978024)
XLA Ops:
  0.0 0.0 copy-start
  0.0 100.0 %whole_step.1 = (f32[768,128]{1,0:T(8,128)S(1)}, f32[128,4096]{1,0:T(8,128)S(1)}) custom-call(f32[768,4096]{1,0:T(8,128)} %matrix_ref.1), custom_call_target="tpu_custom_call" | custom-call | tf_op jit(solution)/shard_map/whole_step/pallas_call | solution.py:353
  100.0 0.0 copy-done
  100.0 8.0 %convolution_subtract_fusion = f32[768,4096]{1,0:T(8,128)} fusion(f32[768,4096]{1,0:T(8,128)S(1)} %copy-done, f32[768,128]{1,0:T(8,128)S(1)} %get-tuple-element.7, f32[128,4096]{1,0:T(8,128)S(1)} %get-tuple-element.8), kind=kOutput, calls=%fused_computation | convolution fusion | flops 2419064832 | bytes 27656192 | tf_op jit(solution)/shard_map/dot_general | solution.py:404
Async XLA Ops:
  0.0 100.0 %copy-start = (f32[768,4096]{1,0:T(8,128)S(1)}, f32[768,4096]{1,0:T(8,128)}, u32[]{:S(2)}) copy-start(f32[768,4096]{1,0:T(8,128)} %matrix_ref.1) | copy-start | bytes 37748740
